TPU v7x, 512 devices: a whole 4x4x16 slice. The times are simulated.
512 devices in a mesh: mesh: 64 (over z_hi, y, x, core), col: 8 (over z_lo).
Axes of the slice: x: 4, y: 4, z: 16 (z_hi: 2, z_lo: 8; z = z_hi * 8 + z_lo), core: 2. Of those that a mesh axis runs over, the one named last changes fastest.
Arguments:
- basis: bfloat16 [786432, 512], P(('mesh', 'col')), may hold values from -24 to 24
- jac_blocks: bfloat16 [12288, 8, 64, 64], P(('mesh', 'col')), may hold values from -0.25 to 0.25
- block_cols: int32 [12288, 8], P(('mesh', 'col')), may hold values from 0 to 12287, as said below
- live_slots: int32 [12288], P(('mesh', 'col')), may hold values from 1 to 8
- accumulation: float32 [786432], P(('mesh', 'col')), may hold values from 0.5 to 4
Outputs:
- image: bfloat16 [786432, 512], P(('mesh', 'col'))
- projected: float32 [512, 512], P('mesh', 'col')
Inputs may be any that keep to these rules, and one draw needn't show every extreme that they name: `block_cols`: each block row's column blocks lie within 2 block rows of it, and some lie exactly 2 away on either side.
All inputs are finite; a program needn't handle non-finite values.
Results may differ from a plain program's by a relative error of at most 0.003.
Values may be sent and summed in bfloat16 or wider, within the bound.
A program may use at most 64 MiB of HBM per device.

v0:
```python
import jax
import jax.numpy as jnp
from jax import lax
from jax.sharding import PartitionSpec as P

REACH = 2


def with_halo(block, sides, width):
    for axis, dim in sides:
        count = lax.axis_size(axis)
        forward = [(i, i + 1) for i in range(count - 1)]
        backward = [(target, source) for source, target in forward]
        low = lax.ppermute(
            lax.slice_in_dim(block, block.shape[dim] - width, None, axis=dim), axis, forward
        )
        high = lax.ppermute(lax.slice_in_dim(block, 0, width, axis=dim), axis, backward)
        block = jnp.concatenate([low, block, high], axis=dim)
    return block


def local(basis, jac_blocks, block_cols, live_slots, accumulation):
    nrows, width = basis.shape
    nblk, slots, bsize, _ = jac_blocks.shape
    padded = with_halo(basis, ((("mesh", "col"), 0),), REACH * bsize)
    first = lax.axis_index(("mesh", "col")) * nblk
    local_cols = block_cols - first + REACH
    pblocks = padded.reshape(nblk + 2 * REACH, bsize, width)
    picked = pblocks[local_cols]
    keep = lax.broadcasted_iota(jnp.int32, (nblk, slots), 1) < live_slots[:, None]
    masked = jnp.where(keep[:, :, None, None], jac_blocks, jnp.zeros_like(jac_blocks))
    coupled = jnp.einsum("rsab,rsbk->rak", masked, picked, preferred_element_type=jnp.float32)
    coupled = coupled.reshape(nrows, width)
    image = (coupled + accumulation[:, None] * basis.astype(jnp.float32)).astype(jnp.bfloat16)
    mesh_count = lax.axis_size("mesh")
    col_count = lax.axis_size("col")
    total_rows = nrows * mesh_count * col_count
    dims = (((0,), (0,)), ((), ()))
    shares = lax.psum_scatter(
        lax.dot_general(basis, image, dims, preferred_element_type=jnp.float32),
        "mesh",
        scatter_dimension=0,
        tiled=True,
    )
    summed = lax.psum_scatter(shares, "col", scatter_dimension=1, tiled=True)
    projected = summed * (1.0 / total_rows)
    return (image, projected)


def solution(mesh):
    return jax.shard_map(
        local,
        mesh=mesh,
        in_specs=(
            P(("mesh", "col"), None),
            P(("mesh", "col"), None, None, None),
            P(("mesh", "col"), None),
            P(("mesh", "col")),
            P(("mesh", "col")),
        ),
        out_specs=(P(("mesh", "col"), None), P("mesh", "col")),
        check_vma=False,
    )
```

profile of v0, /device:TPU:1, one launch (start us, length us, event | category | flops | bytes accessed | tf_op | source)
XLA Modules:
  0.0 681.9 jit_solution(3673218836598132200)
XLA Ops:
  7.2 0.0 reduce-scatter.7.cloned.1.call-start
  7.2 1.0 fusion.6
  8.2 4.4 collective-permute-start
  12.6 11.8 %collective-permute-start.1 = (bf16[128,512]{1,0:T(8,128)(2,1)S(1)}, bf16[128,512]{1,0:T(8,128)(2,1)S(1)}, u32[]{:S(2)}, u32[]{:S(2)}) collective-permute-start(bf16[128,512]{1,0:T(8,128)(2,1)S(1)} %get-tuple-element.9), channel_id=1, source_target_pairs={{1,0},{2,1},{3,2},{4,3},{5,4},{6,5},{7,6},{8,7},{9,8},{10,9},{11,1... | collective-permute-start | bytes 393224 | tf_op jit(solution)/shard_map/ppermute | solution.py:17
  24.4 0.7 compare_select_fusion
  25.1 0.7 iota_compare_fusion
  25.8 0.1 copy.10
  25.9 0.1 reshape.34
  26.0 0.3 collective-permute-done.1
  26.3 1.5 pad_maximum_fusion
  27.9 8.2 %gather_fusion = bf16[192,64,512]{2,1,0:T(8,128)(2,1)} fusion(bf16[28,64,512]{2,1,0:T(8,128)(2,1)S(1)} %bitcast.15, s32[1024]{0:T(1024)S(1)} %pad_clamp_fusion), kind=kCustom, calls=%fused_computation | custom fusion | bytes 25166592 | tf_op jit(solution)/shard_map/gather | solution.py:29
  36.1 8.3 %fusion.1 = f32[24,64,512,1]{2,1,3,0:T(8,128)S(1)} fusion(bf16[24,8,64,512]{3,2,1,0:T(8,128)(2,1)} %bitcast.16, bf16[24,8,64,64]{3,2,1,0:T(8,128)(2,1)} %param.6, pred[24,8]{1,0:T(8,128)(4,1)S(1)} %iota_compare_fusion), kind=kOutput, calls=%fused_computation.3 | convolution fusion | flops 806092800 | bytes 17301696 | tf_op jit(solution)/shard_map/rsab,rsbk->rak/dot_general | solution.py:32
  44.4 0.4 fusion
  44.8 0.0 copy-start.1
  44.8 1.0 convolution_bitcast_fusion
  45.8 1.3 copy.13
  47.1 0.0 reduce-scatter.7.cloned.1.call-update
  47.2 0.0 reduce-scatter.5.cloned.1.call-start
  47.2 564.3 %reduce-scatter.7.cloned.1.call-done = f32[8,512]{1,0:T(8,128)} async-done(((f32[512,512]{1,0:T(8,128)}), f32[8,512]{1,0:T(8,128)}) %reduce-scatter.7.cloned.1.call-update) | async-done | bytes 16400
  611.6 1.6 copy.14
  613.1 0.0 reduce-scatter.5.cloned.1.call-update
  613.1 60.5 %reduce-scatter.5.cloned.1.call-done = f32[8,64]{0,1:T(8,128)} async-done(((f32[8,512]{0,1:T(8,128)}), f32[8,64]{0,1:T(8,128)}) %reduce-scatter.5.cloned.1.call-update) | async-done | bytes 2064 | tf_op jit(solution)/shard_map/reduce_scatter | solution.py:45
  673.7 0.8 broadcast_multiply_fusion
  674.4 0.7 copy.11
  (7 shorter events, 0.0 us)
Async XLA Ops:
  7.2 604.4 %reduce-scatter.7.cloned.1.call-start = ((), (), s32[]{:S(2)}) async-start(), calls=%async_computation.3 | async-start | bytes 1064960
  8.2 17.8 %collective-permute-start = (bf16[128,512]{1,0:T(8,128)(2,1)S(1)}, bf16[128,512]{1,0:T(8,128)(2,1)S(1)}, u32[]{:S(2)}, u32[]{:S(2)}) collective-permute-start(bf16[128,512]{1,0:T(8,128)(2,1)S(1)} %get-tuple-element.8), channel_id=1, source_target_pairs={{0,1},{1,2},{2,3},{3,4},{4,5},{5,6},{6,7},{7,8},{8,9},{9,10},{10,1... | collective-permute-start | bytes 393224 | tf_op jit(solution)/shard_map/ppermute | solution.py:14
  12.6 13.7 %collective-permute-start.1 = (bf16[128,512]{1,0:T(8,128)(2,1)S(1)}, bf16[128,512]{1,0:T(8,128)(2,1)S(1)}, u32[]{:S(2)}, u32[]{:S(2)}) collective-permute-start(bf16[128,512]{1,0:T(8,128)(2,1)S(1)} %get-tuple-element.9), channel_id=1, source_target_pairs={{1,0},{2,1},{3,2},{4,3},{5,4},{6,5},{7,6},{8,7},{9,8},{10,9},{11,1... | collective-permute-start | bytes 393224 | tf_op jit(solution)/shard_map/ppermute | solution.py:17
  36.1 8.3 %copy-start = (bf16[1536,512]{1,0:T(8,128)(2,1)S(1)}, bf16[1536,512]{1,0:T(8,128)(2,1)}, u32[]{:S(2)}) copy-start(bf16[1536,512]{1,0:T(8,128)(2,1)} %param.5) | copy-start | bytes 4718596
  36.1 8.3 %copy-start.2 = (f32[1536]{0:T(1024)S(1)}, f32[1536]{0:T(1024)}, u32[]{:S(2)}) copy-start(f32[1536]{0:T(1024)} %param.9) | copy-start | bytes 18436
  44.8 2.3 copy-start.1
  47.2 626.5 %reduce-scatter.5.cloned.1.call-start = ((), (), s32[]{:S(2)}) async-start(), calls=%async_computation.2 | async-start | bytes 294912 | tf_op jit(solution)/shard_map/reduce_scatter | solution.py:45
Sparse Core Ops, SparseCore 0:
  47.3 564.2 reduce-scatter.6
  614.6 59.0 reduce-scatter.4
where the time goes:
time: 687 us; the launch traced here: 682 us
  waiting for transfers between devices  625 us (91%)
  starting transfers between devices  16.3 us (2%)
  between operations  14.1 us (2%)
  local copies, waits for them, and re-layouts  12.9 us (2%)
  matrix products  9.27 us (1%)
    unnamed x3, waiting for transfers between devices  564 us
    reduce_scatter x1, waiting for transfers between devices, local(): summed = lax.psum_scatter(shares, 'col', scatter_dimension=1, tiled=True)  60.5 us
  transfers between devices with their start and end apart: 4, of which 3 were waited for; matrix products, arithmetic and copies ran while one was open for 0% of the time, Pallas kernels for 0%

commit v1 on v0

--- a/solution.py
+++ b/solution.py
@@ -1,9 +1,15 @@
+import functools
+
 import jax
 import jax.numpy as jnp
 from jax import lax
+from jax.experimental import pallas as pl
+from jax.experimental.pallas import tpu as pltpu
 from jax.sharding import PartitionSpec as P
 
 REACH = 2
+MESH = pl.DeviceIdType.MESH
+NCORE, NX, NY, NZH = 2, 4, 4, 2
 
 
 def with_halo(block, sides, width):
@@ -19,6 +25,110 @@
     return block
 
 
+def scatter_kernel(scale, p_ref, o_ref, pair_in, plane_out, plane_in, line_out, line_in, sems0, s1, r1, s2, r2):
+    m = lax.axis_index("mesh")
+    c = lax.axis_index("col")
+    core = m % NCORE
+    x = (m // NCORE) % NX
+    y = (m // (NCORE * NX)) % NY
+    zh = m // (NCORE * NX * NY)
+    ncol = line_out.shape[0] // NZH
+    nplane, nline = NX * NY, NZH * ncol
+    rows = p_ref.shape[2] // NZH
+    wide = p_ref.shape[3] // ncol
+    z = zh * ncol + c
+
+    def plane_peer(k):
+        px = (x + k % NX) % NX
+        py = (y + k // NX) % NY
+        return py * NX + px, (((zh * NY + py) * NX + px) * NCORE + core, c)
+
+    def line_peer(k):
+        pz = (z + k) % nline
+        return pz, ((pz // ncol) * (NCORE * NX * NY) + m % (NCORE * NX * NY), pz % ncol)
+
+    pair = (m + 1 - 2 * core, c)
+
+    barrier = pltpu.get_barrier_semaphore()
+    pl.semaphore_signal(barrier, inc=1, device_id=pair, device_id_type=MESH)
+    for k in range(1, nplane):
+        pl.semaphore_signal(barrier, inc=1, device_id=plane_peer(k)[1], device_id_type=MESH)
+    for k in range(1, nline):
+        pl.semaphore_signal(barrier, inc=1, device_id=line_peer(k)[1], device_id_type=MESH)
+    pl.semaphore_wait(barrier, 1 + (nplane - 1) + (nline - 1))
+
+    copy0 = pltpu.make_async_remote_copy(
+        src_ref=p_ref.at[1 - core], dst_ref=pair_in, send_sem=sems0.at[0], recv_sem=sems0.at[1],
+        device_id=pair, device_id_type=MESH,
+    )
+    copy0.start()
+    copy0.wait()
+
+    copies1 = []
+    for k in range(1, nplane):
+        j, dev = plane_peer(k)
+        plane_out[j] = (p_ref[core, j].astype(jnp.float32) + pair_in[j].astype(jnp.float32)).astype(plane_out.dtype)
+        copy = pltpu.make_async_remote_copy(
+            src_ref=plane_out.at[j], dst_ref=plane_in.at[k - 1], send_sem=s1.at[k - 1], recv_sem=r1.at[k - 1],
+            device_id=dev, device_id_type=MESH,
+        )
+        copy.start()
+        copies1.append(copy)
+    own = y * NX + x
+    acc = p_ref[core, own].astype(jnp.float32) + pair_in[own].astype(jnp.float32)
+    for k in range(1, nplane):
+        copies1[k - 1].wait_recv()
+        acc += plane_in[k - 1].astype(jnp.float32)
+
+    for h in range(NZH):
+        for q in range(ncol):
+            line_out[h * ncol + q] = acc[h * rows:(h + 1) * rows, q * wide:(q + 1) * wide]
+    copies2 = []
+    for k in range(1, nline):
+        j, dev = line_peer(k)
+        copy = pltpu.make_async_remote_copy(
+            src_ref=line_out.at[j], dst_ref=line_in.at[k - 1], send_sem=s2.at[k - 1], recv_sem=r2.at[k - 1],
+            device_id=dev, device_id_type=MESH,
+        )
+        copy.start()
+        copies2.append(copy)
+    total = line_out[z]
+    for k in range(1, nline):
+        copies2[k - 1].wait_recv()
+        total += line_in[k - 1]
+    o_ref[...] = total * scale
+    for copy in copies1 + copies2:
+        copy.wait_send()
+
+
+def scatter_sum(partial, scale):
+    mesh_count, ncol = lax.axis_size("mesh"), lax.axis_size("col")
+    nrow, ncols = partial.shape
+    rows, wide = nrow // mesh_count, ncols // ncol
+    nplane, nline = NX * NY, NZH * ncol
+    p = partial.reshape(NZH, NY, NX, NCORE, rows, ncols).transpose(3, 1, 2, 0, 4, 5)
+    p = p.reshape(NCORE, nplane, NZH * rows, ncols).astype(jnp.bfloat16)
+    return pl.pallas_call(
+        functools.partial(scatter_kernel, scale),
+        out_shape=jax.ShapeDtypeStruct((rows, wide), jnp.float32),
+        in_specs=[pl.BlockSpec(memory_space=pltpu.VMEM)],
+        out_specs=pl.BlockSpec(memory_space=pltpu.VMEM),
+        scratch_shapes=[
+            pltpu.VMEM((nplane, NZH * rows, ncols), jnp.bfloat16),
+            pltpu.VMEM((nplane, NZH * rows, ncols), jnp.bfloat16),
+            pltpu.VMEM((nplane - 1, NZH * rows, ncols), jnp.bfloat16),
+            pltpu.VMEM((nline, rows, wide), jnp.float32),
+            pltpu.VMEM((nline - 1, rows, wide), jnp.float32),
+            pltpu.SemaphoreType.DMA((2,)),
+            pltpu.SemaphoreType.DMA((nplane - 1,)),
+            pltpu.SemaphoreType.DMA((nplane - 1,)),
+            pltpu.SemaphoreType.DMA((nline - 1,)),
+            pltpu.SemaphoreType.DMA((nline - 1,)),
+        ],
+        compiler_params=pltpu.CompilerParams(collective_id=0, has_side_effects=True),
+    )(p)
+
+
 def local(basis, jac_blocks, block_cols, live_slots, accumulation):
     nrows, width = basis.shape
     nblk, slots, bsize, _ = jac_blocks.shape
@@ -32,18 +142,10 @@
     coupled = jnp.einsum("rsab,rsbk->rak", masked, picked, preferred_element_type=jnp.float32)
     coupled = coupled.reshape(nrows, width)
     image = (coupled + accumulation[:, None] * basis.astype(jnp.float32)).astype(jnp.bfloat16)
-    mesh_count = lax.axis_size("mesh")
-    col_count = lax.axis_size("col")
-    total_rows = nrows * mesh_count * col_count
+    total_rows = nrows * lax.axis_size("mesh") * lax.axis_size("col")
     dims = (((0,), (0,)), ((), ()))
-    shares = lax.psum_scatter(
-        lax.dot_general(basis, image, dims, preferred_element_type=jnp.float32),
-        "mesh",
-        scatter_dimension=0,
-        tiled=True,
-    )
-    summed = lax.psum_scatter(shares, "col", scatter_dimension=1, tiled=True)
-    projected = summed * (1.0 / total_rows)
+    partial = lax.dot_general(basis, image, dims, preferred_element_type=jnp.float32)
+    projected = scatter_sum(partial, 1.0 / total_rows)
     return (image, projected)
 
 

time: 687 us -> 78.4 us (0.11)
  waiting for transfers between devices: 625 us -> 0.31 us
  Pallas kernels: 0 us -> 36.3 us
  between operations: 14.1 us -> 0.74 us
    unnamed x3 -> x0, waiting for transfers between devices: 564 us -> none
    reduce_scatter x1 -> x0, waiting for transfers between devices: 60.5 us -> none  [local(): summed = lax.psum_scatter(shares, 'col', scatter_dimension=1, tiled=True)]
    pallas_call x0 -> x1, Pallas kernels: none -> 36.3 us  [scatter_sum(): pl.pallas_call(functools.partial(scatter_kernel, scale), out_shape=jax.Sh...]
  transfers between devices with their start and end apart: 4 -> 2, of which waited for: 3 -> 1; matrix products, arithmetic and copies ran while one was open for 0% -> 2% of each run, Pallas kernels for 0% -> 0%
where the time goes in v1:
time: 78.4 us; the launch traced here: 77.7 us
  Pallas kernels  36.3 us (46%)
  starting transfers between devices  16.2 us (21%)
  local copies, waits for them, and re-layouts  11.5 us (15%)
  matrix products  9.29 us (12%)
  other arithmetic  3.38 us (4%)
    pallas_call x1, Pallas kernels, scatter_sum(): pl.pallas_call(functools.partial(scatter_kernel, scale), out_shape=jax.Sh...  36.3 us
    ppermute x1, starting transfers between devices, with_halo(): lax.ppermute(lax.slice_in_dim(block, 0, width, axis=dim), axis, backward)  11.8 us
    dot_general x1, matrix products, local(): jnp.einsum('rsab,rsbk->rak', masked, picked, preferred_element_type=jnp.f...  8.27 us
    gather x1, local copies, waits for them, and re-layouts, local(): picked = pblocks[local_cols]  8.23 us
    ppermute x1, starting transfers between devices, with_halo(): lax.ppermute(lax.slice_in_dim(block, block.shape[dim] - width, None, axis...  4.38 us
  transfers between devices with their start and end apart: 2, of which 1 were waited for; matrix products, arithmetic and copies ran while one was open for 2% of the time, Pallas kernels for 0%

profile of v1, /device:TPU:1, one launch (start us, length us, event | category | flops | bytes accessed | tf_op | source)
XLA Modules:
  0.0 77.7 jit_solution(10311348308761516829)
XLA Ops:
  0.6 1.0 %fusion.6 = (bf16[128,512]{1,0:T(8,128)(2,1)S(1)}, bf16[128,512]{1,0:T(8,128)(2,1)S(1)}) fusion(bf16[1536,512]{1,0:T(8,128)(2,1)} %param.5), kind=kLoop, calls=%fused_computation.13 | loop fusion | bytes 524288 | tf_op jit(solution)/shard_map/slice | solution.py:21
  1.6 4.4 %collective-permute-start = (bf16[128,512]{1,0:T(8,128)(2,1)S(1)}, bf16[128,512]{1,0:T(8,128)(2,1)S(1)}, u32[]{:S(2)}, u32[]{:S(2)}) collective-permute-start(bf16[128,512]{1,0:T(8,128)(2,1)S(1)} %get-tuple-element.2), channel_id=1, source_target_pairs={{0,1},{1,2},{2,3},{3,4},{4,5},{5,6},{6,7},{7,8},{8,9},{9,10},{10,1... | collective-permute-start | bytes 393224 | tf_op jit(solution)/shard_map/ppermute | solution.py:20
  6.0 11.8 %collective-permute-start.1 = (bf16[128,512]{1,0:T(8,128)(2,1)S(1)}, bf16[128,512]{1,0:T(8,128)(2,1)S(1)}, u32[]{:S(2)}, u32[]{:S(2)}) collective-permute-start(bf16[128,512]{1,0:T(8,128)(2,1)S(1)} %get-tuple-element.3), channel_id=1, source_target_pairs={{1,0},{2,1},{3,2},{4,3},{5,4},{6,5},{7,6},{8,7},{9,8},{10,9},{11,1... | collective-permute-start | bytes 393224 | tf_op jit(solution)/shard_map/ppermute | solution.py:23
  17.8 0.7 compare_select_fusion
  18.5 0.7 iota_compare_fusion
  19.3 0.1 copy.8
  19.3 0.1 reshape.38
  19.4 0.0 collective-permute-done
  19.4 0.3 collective-permute-done.1
  19.8 1.5 %pad_maximum_fusion = bf16[1792,512]{1,0:T(8,128)(2,1)S(1)} fusion(bf16[128,512]{1,0:T(8,128)(2,1)S(1)} %collective-permute-done.1, bf16[1536,512]{1,0:T(8,128)(2,1)} %param.5, bf16[128,512]{1,0:T(8,128)(2,1)S(1)} %collective-permute-done), kind=kLoop, calls=%fused_computation.6 | loop fusion | flops 5505024 | bytes 3670016 | tf_op jit(solution)/shard_map/concatenate | solution.py:24
  21.3 8.2 %gather_fusion = bf16[192,64,512]{2,1,0:T(8,128)(2,1)} fusion(bf16[28,64,512]{2,1,0:T(8,128)(2,1)S(1)} %bitcast.18, s32[1024]{0:T(1024)S(1)} %pad_clamp_fusion), kind=kCustom, calls=%fused_computation | custom fusion | bytes 25166592 | tf_op jit(solution)/shard_map/gather | solution.py:139
  29.5 0.0 copy-start
  29.5 0.0 copy-start.2
  29.5 8.3 %fusion.1 = f32[24,64,512,1]{2,1,3,0:T(8,128)S(1)} fusion(bf16[24,8,64,512]{3,2,1,0:T(8,128)(2,1)} %bitcast.19, bf16[24,8,64,64]{3,2,1,0:T(8,128)(2,1)} %param.6, pred[24,8]{1,0:T(8,128)(4,1)S(1)} %iota_compare_fusion), kind=kOutput, calls=%fused_computation.3 | convolution fusion | flops 806092800 | bytes 17301696 | tf_op jit(solution)/shard_map/rsab,rsbk->rak/dot_general | solution.py:142
  37.8 0.0 copy-done
  37.8 0.0 copy-done.2
  37.8 0.4 fusion
  38.2 0.0 copy-start.1
  38.3 1.0 %convolution_convert_fusion = bf16[512,512]{0,1:T(8,128)(2,1)S(1)} fusion(bf16[1536,512]{1,0:T(8,128)(2,1)S(1)} %fusion, bf16[1536,512]{1,0:T(8,128)(2,1)S(1)} %copy-done), kind=kOutput, calls=%fused_computation.8 | convolution fusion | flops 805568512 | bytes 3670016 | tf_op jit(solution)/shard_map/dot_general | solution.py:147
  39.3 0.8 %copy.9 = bf16[2,4,4,2,8,512]{5,4,0,2,1,3:T(8,128)(2,1)} copy(bf16[2,4,4,2,8,512]{5,4,3,2,1,0:T(8,128)(2,1)S(1)} %bitcast.21) | data formatting | bytes 1048576 | tf_op jit(solution)/shard_map/convert_element_type | solution.py:110
  40.1 0.0 copy-done.1
  40.1 36.3 %shard_map.68 = f32[8,64]{1,0:T(8,128)} custom-call(bf16[2,16,16,512]{3,2,1,0:T(8,128)(2,1)} %bitcast.20), custom_call_target="tpu_custom_call" | custom-call | tf_op jit(solution)/shard_map/pallas_call | solution.py:111
  76.4 1.3 %copy.12 = f32[8,64]{1,0:T(8,128)} copy(f32[8,64]{1,0:T(8,128)} %shard_map.68) | data formatting | bytes 4096
  (1 shorter events, 0.0 us)
Async XLA Ops:
  1.6 17.8 %collective-permute-start = (bf16[128,512]{1,0:T(8,128)(2,1)S(1)}, bf16[128,512]{1,0:T(8,128)(2,1)S(1)}, u32[]{:S(2)}, u32[]{:S(2)}) collective-permute-start(bf16[128,512]{1,0:T(8,128)(2,1)S(1)} %get-tuple-element.2), channel_id=1, source_target_pairs={{0,1},{1,2},{2,3},{3,4},{4,5},{5,6},{6,7},{7,8},{8,9},{9,10},{10,1... | collective-permute-start | bytes 393224 | tf_op jit(solution)/shard_map/ppermute | solution.py:20
  6.0 13.7 %collective-permute-start.1 = (bf16[128,512]{1,0:T(8,128)(2,1)S(1)}, bf16[128,512]{1,0:T(8,128)(2,1)S(1)}, u32[]{:S(2)}, u32[]{:S(2)}) collective-permute-start(bf16[128,512]{1,0:T(8,128)(2,1)S(1)} %get-tuple-element.3), channel_id=1, source_target_pairs={{1,0},{2,1},{3,2},{4,3},{5,4},{6,5},{7,6},{8,7},{9,8},{10,9},{11,1... | collective-permute-start | bytes 393224 | tf_op jit(solution)/shard_map/ppermute | solution.py:23
  29.5 8.3 %copy-start = (bf16[1536,512]{1,0:T(8,128)(2,1)S(1)}, bf16[1536,512]{1,0:T(8,128)(2,1)}, u32[]{:S(2)}) copy-start(bf16[1536,512]{1,0:T(8,128)(2,1)} %param.5) | copy-start | bytes 4718596
  29.5 8.3 %copy-start.2 = (f32[1536]{0:T(1024)S(1)}, f32[1536]{0:T(1024)}, u32[]{:S(2)}) copy-start(f32[1536]{0:T(1024)} %param.9) | copy-start | bytes 18436
  38.2 1.9 %copy-start.1 = (bf16[1536,512]{1,0:T(8,128)(2,1)}, bf16[1536,512]{1,0:T(8,128)(2,1)S(1)}, u32[]{:S(2)}) copy-start(bf16[1536,512]{1,0:T(8,128)(2,1)S(1)} %fusion) | copy-start | bytes 4718596

commit v2 on v1

--- a/solution.py
+++ b/solution.py
@@ -10,19 +10,16 @@
 REACH = 2
 MESH = pl.DeviceIdType.MESH
 NCORE, NX, NY, NZH = 2, 4, 4, 2
-
-
-def with_halo(block, sides, width):
-    for axis, dim in sides:
-        count = lax.axis_size(axis)
-        forward = [(i, i + 1) for i in range(count - 1)]
-        backward = [(target, source) for source, target in forward]
-        low = lax.ppermute(
-            lax.slice_in_dim(block, block.shape[dim] - width, None, axis=dim), axis, forward
-        )
-        high = lax.ppermute(lax.slice_in_dim(block, 0, width, axis=dim), axis, backward)
-        block = jnp.concatenate([low, block, high], axis=dim)
-    return block
+GROUP = 4
+
+
+def halos(block, axis, width):
+    count = lax.axis_size(axis)
+    forward = [(i, i + 1) for i in range(count - 1)]
+    backward = [(target, source) for source, target in forward]
+    low = lax.ppermute(block[-width:], axis, forward)
+    high = lax.ppermute(block[:width], axis, backward)
+    return low, high
 
 
 def scatter_kernel(scale, p_ref, o_ref, pair_in, plane_out, plane_in, line_out, line_in, sems0, s1, r1, s2, r2):
@@ -101,22 +98,123 @@
         copy.wait_send()
 
 
-def scatter_sum(partial, scale):
-    mesh_count, ncol = lax.axis_size("mesh"), lax.axis_size("col")
-    nrow, ncols = partial.shape
-    rows, wide = nrow // mesh_count, ncols // ncol
-    nplane, nline = NX * NY, NZH * ncol
-    p = partial.reshape(NZH, NY, NX, NCORE, rows, ncols).transpose(3, 1, 2, 0, 4, 5)
-    p = p.reshape(NCORE, nplane, NZH * rows, ncols).astype(jnp.bfloat16)
+def dense_kernel(low_ref, basis_ref, high_ref, jac_ref, cols_ref, live_ref, acc_ref, image_ref, part_ref, pad, top, rest, sem):
+    nblk, slots, bs, _ = jac_ref.shape
+    width = basis_ref.shape[1]
+    reach = low_ref.shape[0]
+    nrows = nblk * bs
+    span = GROUP * bs + 2 * reach
+    lanes = 2 * bs
+    first = (lax.axis_index("mesh") * lax.axis_size("col") + lax.axis_index("col")) * nblk
+    moves = [
+        pltpu.make_async_copy(low_ref, pad.at[pl.ds(0, reach)], sem.at[0]),
+        pltpu.make_async_copy(basis_ref, pad.at[pl.ds(reach, nrows)], sem.at[1]),
+        pltpu.make_async_copy(high_ref, pad.at[pl.ds(reach + nrows, reach)], sem.at[2]),
+    ]
+    for move in moves:
+        move.start()
+    left = lax.broadcasted_iota(jnp.int32, (1, lanes), 1) < bs
+    lane = lax.broadcasted_iota(jnp.int32, (bs, lanes), 1)
+    row = lax.broadcasted_iota(jnp.int32, (bs, lanes), 0)
+
+    def build(g, carry):
+        for i in range(GROUP):
+            r = g * GROUP + i
+            own = first + r
+            place = [jnp.where(s < live_ref[r], cols_ref[s, r] - own + REACH, -slots) for s in range(slots)]
+            tiles = [jnp.zeros((bs, lanes), jnp.float32) for _ in range(3)]
+            for p in range(0, slots, 2):
+                a, b = jac_ref[r, p], jac_ref[r, p + 1]
+                straight = jnp.concatenate([a, b], axis=1).astype(jnp.float32)
+                crossed = jnp.concatenate([b, a], axis=1).astype(jnp.float32)
+                where_s = jnp.where(left, place[p], place[p + 1])
+                where_c = jnp.where(left, place[p + 1], place[p])
+                for t in range(3):
+                    w = 2 * (t + i // 2) - i
+                    goal = jnp.where(left, w, w + 1)
+                    tiles[t] += straight * (where_s == goal).astype(jnp.float32)
+                    tiles[t] += crossed * (where_c == goal).astype(jnp.float32)
+            t = (i + REACH) // 2 - i // 2
+            gains = acc_ref[pl.ds(g * (GROUP // 2) + i // 2, 1), :]
+            tiles[t] += jnp.where(lane == row + bs * (i % 2), gains, 0.0)
+            for t in range(span // lanes):
+                k = t - i // 2
+                here = (g, pl.ds(i * bs, bs), pl.ds(t * lanes, lanes))
+                if 0 <= k < 3:
+                    big = tiles[k].astype(jnp.bfloat16)
+                    top[here] = big
+                    rest[here] = (tiles[k] - big.astype(jnp.float32)).astype(jnp.bfloat16)
+                else:
+                    top[here] = jnp.zeros((bs, lanes), jnp.bfloat16)
+                    rest[here] = jnp.zeros((bs, lanes), jnp.bfloat16)
+        return carry
+
+    lax.fori_loop(0, nblk // GROUP, build, 0)
+    for move in moves:
+        move.wait()
+
+    def apply(g, carry):
+        rows = GROUP * bs
+        window = pad[pl.ds(pl.multiple_of(g * rows, rows), span), :]
+        out = jnp.dot(top[g], window, preferred_element_type=jnp.float32)
+        out += jnp.dot(rest[g], window, preferred_element_type=jnp.float32)
+        image_ref[pl.ds(pl.multiple_of(g * rows, rows), rows), :] = out.astype(image_ref.dtype)
+        return carry
+
+    lax.fori_loop(0, nblk // GROUP, apply, 0)
+
+    part = lax.dot_general(
+        pad[pl.ds(reach, nrows), :], image_ref[...], (((0,), (0,)), ((), ())), preferred_element_type=jnp.float32
+    )
+    ncore, nplane, both, _ = part_ref.shape
+    rows = both // NZH
+    for core in range(ncore):
+        for j in range(nplane):
+            for h in range(NZH):
+                at = ((h * nplane + j) * ncore + core) * rows
+                part_ref[core, j, h * rows:(h + 1) * rows] = part[at:at + rows].astype(part_ref.dtype)
+
+
+def dense(basis, low, high, jac_blocks, block_cols, live_slots, accumulation):
+    nrows, width = basis.shape
+    nblk, slots, bs, _ = jac_blocks.shape
+    nplane = NX * NY
+    rows = width // lax.axis_size("mesh")
+    span = (GROUP + 2 * REACH) * bs
+    ngroup = nblk // GROUP
+    any_spec = pl.BlockSpec(memory_space=pl.ANY)
+    vmem = pl.BlockSpec(memory_space=pltpu.VMEM)
+    smem = pl.BlockSpec(memory_space=pltpu.SMEM)
+    return pl.pallas_call(
+        dense_kernel,
+        out_shape=(
+            jax.ShapeDtypeStruct((nrows, width), jnp.bfloat16),
+            jax.ShapeDtypeStruct((NCORE, nplane, NZH * rows, width), jnp.bfloat16),
+        ),
+        in_specs=[any_spec, any_spec, any_spec, vmem, smem, smem, vmem],
+        out_specs=(vmem, vmem),
+        scratch_shapes=[
+            pltpu.VMEM((nrows + 2 * REACH * bs, width), jnp.bfloat16),
+            pltpu.VMEM((ngroup, GROUP * bs, span), jnp.bfloat16),
+            pltpu.VMEM((ngroup, GROUP * bs, span), jnp.bfloat16),
+            pltpu.SemaphoreType.DMA((3,)),
+        ],
+        compiler_params=pltpu.CompilerParams(vmem_limit_bytes=40 << 20),
+    )(low, basis, high, jac_blocks, block_cols.T, live_slots, accumulation.reshape(nrows // (2 * bs), 2 * bs))
+
+
+def scatter_sum(p, scale, rows, wide):
+    ncore, nplane, both, ncols = p.shape
+    nline = NZH * (ncols // wide)
     return pl.pallas_call(
         functools.partial(scatter_kernel, scale),
         out_shape=jax.ShapeDtypeStruct((rows, wide), jnp.float32),
         in_specs=[pl.BlockSpec(memory_space=pltpu.VMEM)],
         out_specs=pl.BlockSpec(memory_space=pltpu.VMEM),
         scratch_shapes=[
-            pltpu.VMEM((nplane, NZH * rows, ncols), jnp.bfloat16),
-            pltpu.VMEM((nplane, NZH * rows, ncols), jnp.bfloat16),
-            pltpu.VMEM((nplane - 1, NZH * rows, ncols), jnp.bfloat16),
+            pltpu.VMEM((nplane, both, ncols), jnp.bfloat16),
+            pltpu.VMEM((nplane, both, ncols), jnp.bfloat16),
+            pltpu.VMEM((nplane - 1, both, ncols), jnp.bfloat16),
             pltpu.VMEM((nline, rows, wide), jnp.float32),
             pltpu.VMEM((nline - 1, rows, wide), jnp.float32),
             pltpu.SemaphoreType.DMA((2,)),
@@ -131,21 +229,12 @@
 
 def local(basis, jac_blocks, block_cols, live_slots, accumulation):
     nrows, width = basis.shape
-    nblk, slots, bsize, _ = jac_blocks.shape
-    padded = with_halo(basis, ((("mesh", "col"), 0),), REACH * bsize)
-    first = lax.axis_index(("mesh", "col")) * nblk
-    local_cols = block_cols - first + REACH
-    pblocks = padded.reshape(nblk + 2 * REACH, bsize, width)
-    picked = pblocks[local_cols]
-    keep = lax.broadcasted_iota(jnp.int32, (nblk, slots), 1) < live_slots[:, None]
-    masked = jnp.where(keep[:, :, None, None], jac_blocks, jnp.zeros_like(jac_blocks))
-    coupled = jnp.einsum("rsab,rsbk->rak", masked, picked, preferred_element_type=jnp.float32)
-    coupled = coupled.reshape(nrows, width)
-    image = (coupled + accumulation[:, None] * basis.astype(jnp.float32)).astype(jnp.bfloat16)
-    total_rows = nrows * lax.axis_size("mesh") * lax.axis_size("col")
-    dims = (((0,), (0,)), ((), ()))
-    partial = lax.dot_general(basis, image, dims, preferred_element_type=jnp.float32)
-    projected = scatter_sum(partial, 1.0 / total_rows)
+    bs = jac_blocks.shape[2]
+    mesh_count, col_count = lax.axis_size("mesh"), lax.axis_size("col")
+    low, high = halos(basis, ("mesh", "col"), REACH * bs)
+    image, part = dense(basis, low, high, jac_blocks, block_cols, live_slots, accumulation)
+    scale = 1.0 / (nrows * mesh_count * col_count)
+    projected = scatter_sum(part, scale, width // mesh_count, width // col_count)
     return (image, projected)
 
 

time: 78.4 us -> 73 us (0.931)
  waiting for transfers between devices: 0.31 us -> 12.3 us
  matrix products: 9.29 us -> 0 us
  other arithmetic: 3.38 us -> 0 us
  local copies, waits for them, and re-layouts: 11.5 us -> 8.38 us
  Pallas kernels: 36.3 us -> 35 us
    ppermute x2, waiting for transfers between devices: 0.31 us -> 12.3 us  [the longest x1 12.3 us: halos(): low = lax.ppermute(block[-width:], axis, forward)]
    dot_general x2 -> x0, matrix products: 9.29 us -> none  [the longest x1 8.27 us: local(): jnp.einsum('rsab,rsbk->rak', masked, picked, preferred_element_type=jnp.f...]
    pallas_call x1, Pallas kernels: 36.3 us -> 27.6 us  [scatter_sum(): pl.pallas_call(functools.partial(scatter_kernel, scale), out_shape=jax.Sh...]
    gather x1 -> x0, local copies, waits for them, and re-layouts: 8.23 us -> none  [local(): picked = pblocks[local_cols]]
    pallas_call x0 -> x1, Pallas kernels: none -> 7.38 us  [dense(): pl.pallas_call(dense_kernel, out_shape=(jax.ShapeDtypeStruct((nrows, widt...]
    unnamed x7 -> x13, local copies, waits for them, and re-layouts: 1.28 us -> 7.39 us
    concatenate x1 -> x0, other arithmetic: 1.53 us -> none  [with_halo(): block = jnp.concatenate([low, block, high], axis=dim)]
    convert_element_type x1 -> x0, local copies, waits for them, and re-layouts: 0.85 us -> none  [scatter_sum(): p = p.reshape(NCORE, nplane, NZH * rows, ncols).astype(jnp.bfloat16)]
  transfers between devices with their start and end apart: 2 -> 2, of which waited for: 1 -> 1; matrix products, arithmetic and copies ran while one was open for 2% -> 0% of each run, Pallas kernels for 0% -> 0%
where the time goes in v2:
time: 73 us; the launch traced here: 72.6 us
  Pallas kernels  35 us (48%)
  starting transfers between devices  16.2 us (22%)
  waiting for transfers between devices  12.3 us (17%)
  local copies, waits for them, and re-layouts  8.38 us (11%)
    pallas_call x1, Pallas kernels, scatter_sum(): pl.pallas_call(functools.partial(scatter_kernel, scale), out_shape=jax.Sh...  27.6 us
    ppermute x1, starting transfers between devices, halos(): high = lax.ppermute(block[:width], axis, backward)  14.3 us
    ppermute x1, waiting for transfers between devices, halos(): low = lax.ppermute(block[-width:], axis, forward)  12.3 us
    unnamed x13, local copies, waits for them, and re-layouts  7.39 us
    pallas_call x1, Pallas kernels, dense(): pl.pallas_call(dense_kernel, out_shape=(jax.ShapeDtypeStruct((nrows, widt...  7.38 us
    ppermute x1, starting transfers between devices, halos(): low = lax.ppermute(block[-width:], axis, forward)  1.92 us
  transfers between devices with their start and end apart: 2, of which 1 were waited for; matrix products, arithmetic and copies ran while one was open for 0% of the time, Pallas kernels for 0%

profile of v2, /device:TPU:1, one launch (start us, length us, event | category | flops | bytes accessed | tf_op | source)
XLA Modules:
  0.0 72.6 jit_solution(8905791779397818561)
XLA Ops:
  0.6 1.0 %fusion = (bf16[128,512]{1,0:T(8,128)(2,1)S(1)}, bf16[128,512]{1,0:T(8,128)(2,1)S(1)}) fusion(bf16[1536,512]{1,0:T(8,128)(2,1)} %basis_ref.1), kind=kLoop, calls=%fused_computation | loop fusion | bytes 524288 | tf_op jit(solution)/shard_map/slice | solution.py:21
  1.6 14.3 %collective-permute-start.1 = (bf16[128,512]{1,0:T(8,128)(2,1)S(1)}, bf16[128,512]{1,0:T(8,128)(2,1)S(1)}, u32[]{:S(2)}, u32[]{:S(2)}) collective-permute-start(bf16[128,512]{1,0:T(8,128)(2,1)S(1)} %get-tuple-element.6), channel_id=1, source_target_pairs={{1,0},{2,1},{3,2},{4,3},{5,4},{6,5},{7,6},{8,7},{9,8},{10,9},{11,1... | collective-permute-start | bytes 393224 | tf_op jit(solution)/shard_map/ppermute | solution.py:21
  15.9 1.9 %collective-permute-start = (bf16[128,512]{1,0:T(8,128)(2,1)S(1)}, bf16[128,512]{1,0:T(8,128)(2,1)S(1)}, u32[]{:S(2)}, u32[]{:S(2)}) collective-permute-start(bf16[128,512]{1,0:T(8,128)(2,1)S(1)} %get-tuple-element.7), channel_id=1, source_target_pairs={{0,1},{1,2},{2,3},{3,4},{4,5},{5,6},{6,7},{7,8},{8,9},{9,10},{10,1... | collective-permute-start | bytes 393224 | tf_op jit(solution)/shard_map/ppermute | solution.py:20
  17.8 0.0 collective-permute-done.1.high_ref
  17.8 12.3 %collective-permute-done.low_ref = bf16[128,512]{1,0:T(8,128)(2,1)S(1)} collective-permute-done((bf16[128,512]{1,0:T(8,128)(2,1)S(1)}, bf16[128,512]{1,0:T(8,128)(2,1)S(1)}, u32[]{:S(2)}, u32[]{:S(2)}) %collective-permute-start) | collective-permute-done | bytes 131104 | tf_op jit(solution)/shard_map/ppermute | solution.py:20
  30.1 0.0 copy-start
  30.1 1.9 %copy-done = bf16[24,8,64,64]{3,2,1,0:T(8,128)(2,1)S(1)} copy-done((bf16[24,8,64,64]{3,2,1,0:T(8,128)(2,1)S(1)}, bf16[24,8,64,64]{3,2,1,0:T(8,128)(2,1)}, u32[]{:S(2)}) %copy-start) | copy-done | bytes 1572888
  32.0 0.0 copy-start.1
  32.0 1.4 %copy-done.1 = bf16[1536,512]{1,0:T(8,128)(2,1)S(1)} copy-done((bf16[1536,512]{1,0:T(8,128)(2,1)S(1)}, bf16[1536,512]{1,0:T(8,128)(2,1)}, u32[]{:S(2)}) %copy-start.1) | copy-done | bytes 1572888
  33.4 0.0 copy-start.3
  33.4 0.7 copy-done.3
  34.1 0.0 copy-start.4
  34.1 0.7 copy-done.4
  34.8 0.0 copy-start.5
  34.8 0.7 copy-done.5
  35.5 7.4 %shard_map.68 = (bf16[1536,512]{1,0:T(8,128)(2,1)}, bf16[2,16,16,512]{3,2,1,0:T(8,128)(2,1)S(1)}) custom-call(bf16[128,512]{1,0:T(8,128)(2,1)S(1)} %collective-permute-done.low_ref, bf16[1536,512]{1,0:T(8,128)(2,1)S(1)} %copy-done.1, bf16[128,512]{1,0:T(8,128)(2,1)S(1)} %collective-permute-done.1.high_ref, bf16[24,8,64,64]{3,2,1,0:T(8,128)(2,1)S(1)} %copy-done, ...), custom_call_target="tpu_custom_call" | custom-call | tf_op jit(solution)/shard_map/pallas_call | solution.py:188
  42.9 0.0 copy-start.2
  42.9 0.8 %copy-done.2 = bf16[2,16,16,512]{3,2,1,0:T(8,128)(2,1)} copy-done((bf16[2,16,16,512]{3,2,1,0:T(8,128)(2,1)}, bf16[2,16,16,512]{3,2,1,0:T(8,128)(2,1)S(1)}, u32[]{:S(2)}) %copy-start.2) | copy-done | bytes 524312
  43.7 27.6 %shard_map.69 = f32[8,64]{1,0:T(8,128)} custom-call(bf16[2,16,16,512]{3,2,1,0:T(8,128)(2,1)} %copy-done.2), custom_call_target="tpu_custom_call" | custom-call | tf_op jit(solution)/shard_map/pallas_call | solution.py:209
  71.3 1.3 %copy.8 = f32[8,64]{1,0:T(8,128)} copy(f32[8,64]{1,0:T(8,128)} %shard_map.69) | data formatting | bytes 4096
Async XLA Ops:
  1.6 16.2 %collective-permute-start.1 = (bf16[128,512]{1,0:T(8,128)(2,1)S(1)}, bf16[128,512]{1,0:T(8,128)(2,1)S(1)}, u32[]{:S(2)}, u32[]{:S(2)}) collective-permute-start(bf16[128,512]{1,0:T(8,128)(2,1)S(1)} %get-tuple-element.6), channel_id=1, source_target_pairs={{1,0},{2,1},{3,2},{4,3},{5,4},{6,5},{7,6},{8,7},{9,8},{10,9},{11,1... | collective-permute-start | bytes 393224 | tf_op jit(solution)/shard_map/ppermute | solution.py:21
  15.9 14.3 %collective-permute-start = (bf16[128,512]{1,0:T(8,128)(2,1)S(1)}, bf16[128,512]{1,0:T(8,128)(2,1)S(1)}, u32[]{:S(2)}, u32[]{:S(2)}) collective-permute-start(bf16[128,512]{1,0:T(8,128)(2,1)S(1)} %get-tuple-element.7), channel_id=1, source_target_pairs={{0,1},{1,2},{2,3},{3,4},{4,5},{5,6},{6,7},{7,8},{8,9},{9,10},{10,1... | collective-permute-start | bytes 393224 | tf_op jit(solution)/shard_map/ppermute | solution.py:20
  30.1 1.9 %copy-start = (bf16[24,8,64,64]{3,2,1,0:T(8,128)(2,1)S(1)}, bf16[24,8,64,64]{3,2,1,0:T(8,128)(2,1)}, u32[]{:S(2)}) copy-start(bf16[24,8,64,64]{3,2,1,0:T(8,128)(2,1)} %jac_ref.1) | copy-start | bytes 4718596
  32.0 1.4 %copy-start.1 = (bf16[1536,512]{1,0:T(8,128)(2,1)S(1)}, bf16[1536,512]{1,0:T(8,128)(2,1)}, u32[]{:S(2)}) copy-start(bf16[1536,512]{1,0:T(8,128)(2,1)} %basis_ref.1) | copy-start | bytes 4718596
  33.4 0.7 copy-start.3
  34.1 0.7 copy-start.4
  34.8 0.7 copy-start.5
  42.9 0.8 %copy-start.2 = (bf16[2,16,16,512]{3,2,1,0:T(8,128)(2,1)}, bf16[2,16,16,512]{3,2,1,0:T(8,128)(2,1)S(1)}, u32[]{:S(2)}) copy-start(bf16[2,16,16,512]{3,2,1,0:T(8,128)(2,1)S(1)} %get-tuple-element.5.p_ref) | copy-start | bytes 1572868

commit v3 on v0

v3 whole, which is shorter than its diff:
```python
import functools

import jax
import jax.numpy as jnp
from jax import lax
from jax.experimental import pallas as pl
from jax.experimental.pallas import tpu as pltpu
from jax.sharding import PartitionSpec as P

REACH = 2
GROUP = 4
MESH = pl.DeviceIdType.MESH
NCORE, NX, NY, NZH = 2, 4, 4, 2
PIECES = 4


def hops(step, size):
    return min(step, size - step)


PLANE = sorted(
    ((dx, dy) for dx in range(NX) for dy in range(NY)), key=lambda d: -hops(d[0], NX) - hops(d[1], NY)
)


def kernel(
    basis_ref, jac_ref, cols_ref, live_ref, acc_ref, image_ref, total_ref,
    pad, jac, cols, live, gain, top, rest, part, pair_out, pair_in, plane_out, plane_in, line_out, line_in,
    local_sem, halo_send, halo_recv, s0, r0, s1, r1, s2, r2,
):
    m, c = lax.axis_index("mesh"), lax.axis_index("col")
    nm, nc = lax.axis_size("mesh"), lax.axis_size("col")
    core = m % NCORE
    x = (m // NCORE) % NX
    y = (m // (NCORE * NX)) % NY
    zh = m // (NCORE * NX * NY)
    z = zh * nc + c
    nplane, nline = NX * NY, NZH * nc
    line_steps = sorted(range(1, nline), key=lambda k: -hops(k, nline))

    nblk, slots, bs, _ = jac.shape
    nrows, width = basis_ref.shape
    reach = REACH * bs
    span = GROUP * bs + 2 * reach
    lanes = 2 * bs
    rows = total_ref.shape[0]
    wide = total_ref.shape[1]

    def plane_peer(step):
        px, py = (x + step[0]) % NX, (y + step[1]) % NY
        return py * NX + px, (((zh * NY + py) * NX + px) * NCORE + core, c)

    def line_peer(k):
        pz = (z + k) % nline
        return pz, ((pz // nc) * (NCORE * NX * NY) + m % (NCORE * NX * NY), pz % nc)

    index = m * nc + c
    before, after = (index + nm * nc - 1) % (nm * nc), (index + 1) % (nm * nc)
    low_peer, high_peer = (before // nc, before % nc), (after // nc, after % nc)
    pair = (m + 1 - 2 * core, c)

    moves = [
        pltpu.make_async_copy(cols_ref, cols, local_sem.at[0]),
        pltpu.make_async_copy(live_ref, live, local_sem.at[1]),
        pltpu.make_async_copy(acc_ref, gain, local_sem.at[2]),
        pltpu.make_async_copy(jac_ref, jac, local_sem.at[3]),
        pltpu.make_async_copy(basis_ref, pad.at[pl.ds(reach, nrows)], local_sem.at[4]),
    ]
    for move in moves:
        move.start()

    barrier = pltpu.get_barrier_semaphore()
    peers = [low_peer, high_peer] + [line_peer(k)[1] for k in line_steps]
    peers += [plane_peer(step)[1] for step in PLANE[:-1]] + [pair]
    for peer in peers:
        pl.semaphore_signal(barrier, inc=1, device_id=peer, device_id_type=MESH)

    for move in moves[:4]:
        move.wait()

    first = index * nblk
    left = lax.broadcasted_iota(jnp.int32, (1, lanes), 1) < bs
    lane = lax.broadcasted_iota(jnp.int32, (bs, lanes), 1)
    row = lax.broadcasted_iota(jnp.int32, (bs, lanes), 0)

    def build(g, carry):
        for i in range(GROUP):
            r = g * GROUP + i
            own = first + r
            place = [jnp.where(s < live[r], cols[s, r] - own + REACH, -slots) for s in range(slots)]
            tiles = [jnp.zeros((bs, lanes), jnp.float32) for _ in range(3)]
            for p in range(0, slots, 2):
                a, b = jac[r, p], jac[r, p + 1]
                straight = jnp.concatenate([a, b], axis=1).astype(jnp.float32)
                crossed = jnp.concatenate([b, a], axis=1).astype(jnp.float32)
                where_s = jnp.where(left, place[p], place[p + 1])
                where_c = jnp.where(left, place[p + 1], place[p])
                for t in range(3):
                    w = 2 * (t + i // 2) - i
                    goal = jnp.where(left, w, w + 1)
                    tiles[t] += straight * (where_s == goal).astype(jnp.float32)
                    tiles[t] += crossed * (where_c == goal).astype(jnp.float32)
            t = (i + REACH) // 2 - i // 2
            gains = gain[pl.ds(g * (GROUP // 2) + i // 2, 1), :]
            tiles[t] += jnp.where(lane == row + bs * (i % 2), gains, 0.0)
            for t in range(span // lanes):
                k = t - i // 2
                here = (g, pl.ds(i * bs, bs), pl.ds(t * lanes, lanes))
                if 0 <= k < 3:
                    big = tiles[k].astype(jnp.bfloat16)
                    top[here] = big
                    rest[here] = (tiles[k] - big.astype(jnp.float32)).astype(jnp.bfloat16)
                else:
                    top[here] = jnp.zeros((bs, lanes), jnp.bfloat16)
                    rest[here] = jnp.zeros((bs, lanes), jnp.bfloat16)
        return carry

    ngroup = nblk // GROUP
    lax.fori_loop(0, ngroup, build, 0)
    moves[4].wait()

    pl.semaphore_wait(barrier, len(peers))
    up = pltpu.make_async_remote_copy(
        src_ref=pad.at[pl.ds(nrows, reach)], dst_ref=pad.at[pl.ds(0, reach)],
        send_sem=halo_send.at[0], recv_sem=halo_recv.at[0], device_id=high_peer, device_id_type=MESH,
    )
    down = pltpu.make_async_remote_copy(
        src_ref=pad.at[pl.ds(reach, reach)], dst_ref=pad.at[pl.ds(reach + nrows, reach)],
        send_sem=halo_send.at[1], recv_sem=halo_recv.at[1], device_id=low_peer, device_id_type=MESH,
    )
    up.start()
    down.start()

    step = GROUP * bs

    def apply(g, carry):
        at = pl.multiple_of(g * step, step)
        window = pad[pl.ds(at, span), :]
        out = jnp.dot(top[g], window, preferred_element_type=jnp.float32)
        out += jnp.dot(rest[g], window, preferred_element_type=jnp.float32)
        image_ref[pl.ds(at, step), :] = out.astype(image_ref.dtype)
        return carry

    def project(start, size):
        return lax.dot_general(
            pad[pl.ds(reach + start, size), :], image_ref[pl.ds(start, size), :],
            (((0,), (0,)), ((), ())), preferred_element_type=jnp.float32,
        )

    lax.fori_loop(1, ngroup - 1, apply, 0)
    part[...] = project(step, nrows - 2 * step)
    up.wait()
    down.wait()
    apply(0, 0)
    apply(ngroup - 1, 0)
    part[...] += project(0, step) + project(nrows - step, step)

    def share(j, which):
        at = [pl.multiple_of(((h * nplane + j) * NCORE + which) * rows, rows) for h in range(NZH)]
        return jnp.concatenate([part[pl.ds(a, rows), :] for a in at], axis=0)

    each = nplane // PIECES
    swaps = []
    for q in range(PIECES):
        for n in range(q * each, (q + 1) * each):
            pair_out[n] = share(plane_peer(PLANE[n])[0], 1 - core).astype(pair_out.dtype)
        swap = pltpu.make_async_remote_copy(
            src_ref=pair_out.at[pl.ds(q * each, each)], dst_ref=pair_in.at[pl.ds(q * each, each)],
            send_sem=s0.at[q], recv_sem=r0.at[q], device_id=pair, device_id_type=MESH,
        )
        swap.start()
        swaps.append(swap)

    sent = []
    acc = None
    for q in range(PIECES):
        swaps[q].wait_recv()
        for n in range(q * each, (q + 1) * each):
            j, peer = plane_peer(PLANE[n])
            both = share(j, core) + pair_in[n].astype(jnp.float32)
            if n == nplane - 1:
                acc = both
                continue
            plane_out[n] = both.astype(plane_out.dtype)
            copy = pltpu.make_async_remote_copy(
                src_ref=plane_out.at[n], dst_ref=plane_in.at[n], send_sem=s1.at[n], recv_sem=r1.at[n],
                device_id=peer, device_id_type=MESH,
            )
            copy.start()
            sent.append(copy)
    for n in reversed(range(nplane - 1)):
        sent[n].wait_recv()
        acc += plane_in[n].astype(jnp.float32)

    for h in range(NZH):
        for q in range(nc):
            line_out[h * nc + q] = acc[h * rows:(h + 1) * rows, q * wide:(q + 1) * wide]
    last = []
    for n, k in enumerate(line_steps):
        j, peer = line_peer(k)
        copy = pltpu.make_async_remote_copy(
            src_ref=line_out.at[j], dst_ref=line_in.at[n], send_sem=s2.at[n], recv_sem=r2.at[n],
            device_id=peer, device_id_type=MESH,
        )
        copy.start()
        last.append(copy)
    total = line_out[z]
    for n in reversed(range(nline - 1)):
        last[n].wait_recv()
        total += line_in[n]
    total_ref[...] = total
    for copy in swaps + sent + last:
        copy.wait_send()


def local(basis, jac_blocks, block_cols, live_slots, accumulation):
    nrows, width = basis.shape
    nblk, slots, bs, _ = jac_blocks.shape
    mesh_count, col_count = lax.axis_size("mesh"), lax.axis_size("col")
    rows, wide = width // mesh_count, width // col_count
    nplane, nline = NX * NY, NZH * col_count
    span = (GROUP + 2 * REACH) * bs
    ngroup = nblk // GROUP
    lanes = 2 * bs
    image, total = pl.pallas_call(
        kernel,
        out_shape=(
            jax.ShapeDtypeStruct((nrows, width), jnp.bfloat16),
            jax.ShapeDtypeStruct((rows, wide), jnp.float32),
        ),
        in_specs=[pl.BlockSpec(memory_space=pl.ANY)] * 5,
        out_specs=(pl.BlockSpec(memory_space=pltpu.VMEM), pl.BlockSpec(memory_space=pltpu.VMEM)),
        scratch_shapes=[
            pltpu.VMEM((nrows + 2 * REACH * bs, width), jnp.bfloat16),
            pltpu.VMEM((nblk, slots, bs, bs), jnp.bfloat16),
            pltpu.SMEM((slots, nblk), jnp.int32),
            pltpu.SMEM((nblk,), jnp.int32),
            pltpu.VMEM((nrows // lanes, lanes), jnp.float32),
            pltpu.VMEM((ngroup, GROUP * bs, span), jnp.bfloat16),
            pltpu.VMEM((ngroup, GROUP * bs, span), jnp.bfloat16),
            pltpu.VMEM((width, width), jnp.float32),
            pltpu.VMEM((nplane, NZH * rows, width), jnp.bfloat16),
            pltpu.VMEM((nplane, NZH * rows, width), jnp.bfloat16),
            pltpu.VMEM((nplane - 1, NZH * rows, width), jnp.bfloat16),
            pltpu.VMEM((nplane - 1, NZH * rows, width), jnp.bfloat16),
            pltpu.VMEM((nline, rows, wide), jnp.float32),
            pltpu.VMEM((nline - 1, rows, wide), jnp.float32),
            pltpu.SemaphoreType.DMA((5,)),
            pltpu.SemaphoreType.DMA((2,)),
            pltpu.SemaphoreType.DMA((2,)),
            pltpu.SemaphoreType.DMA((PIECES,)),
            pltpu.SemaphoreType.DMA((PIECES,)),
            pltpu.SemaphoreType.DMA((nplane - 1,)),
            pltpu.SemaphoreType.DMA((nplane - 1,)),
            pltpu.SemaphoreType.DMA((nline - 1,)),
            pltpu.SemaphoreType.DMA((nline - 1,)),
        ],
        compiler_params=pltpu.CompilerParams(
            collective_id=0, has_side_effects=True, vmem_limit_bytes=56 << 20
        ),
    )(basis, jac_blocks, block_cols.T, live_slots, accumulation.reshape(nrows // lanes, lanes))
    projected = total * (1.0 / (nrows * mesh_count * col_count))
    return (image, projected)


def solution(mesh):
    return jax.shard_map(
        local,
        mesh=mesh,
        in_specs=(
            P(("mesh", "col"), None),
            P(("mesh", "col"), None, None, None),
            P(("mesh", "col"), None),
            P(("mesh", "col")),
            P(("mesh", "col")),
        ),
        out_specs=(P(("mesh", "col"), None), P("mesh", "col")),
        check_vma=False,
    )
```

time: 687 us -> 47.4 us (0.07)
  waiting for transfers between devices: 625 us -> 0 us
  Pallas kernels: 0 us -> 42.6 us
  starting transfers between devices: 16.3 us -> 0 us
  between operations: 14.1 us -> 0.64 us
  local copies, waits for them, and re-layouts: 12.9 us -> 2.65 us
  matrix products: 9.27 us -> 0 us
    unnamed x3 -> x0, waiting for transfers between devices: 564 us -> none
    reduce_scatter x1 -> x0, waiting for transfers between devices: 60.5 us -> none  [local(): summed = lax.psum_scatter(shares, 'col', scatter_dimension=1, tiled=True)]
    pallas_call x0 -> x1, Pallas kernels: none -> 42.6 us  [local(): pl.pallas_call(kernel, out_shape=(jax.ShapeDtypeStruct((nrows, width), jn...]
    ppermute x2 -> x0, starting transfers between devices: 16.2 us -> none  [the longest x1 11.8 us: with_halo(): lax.ppermute(lax.slice_in_dim(block, 0, width, axis=dim), axis, backward)]
    dot_general x2 -> x0, matrix products: 9.27 us -> none  [the longest x1 8.27 us: local(): jnp.einsum('rsab,rsbk->rak', masked, picked, preferred_element_type=jnp.f...]
    gather x1 -> x0, local copies, waits for them, and re-layouts: 8.23 us -> none  [local(): picked = pblocks[local_cols]]
  transfers between devices with their start and end apart: 4 -> 0, of which waited for: 3 -> 0; matrix products, arithmetic and copies ran while one was open for 0% -> 0% of each run, Pallas kernels for 0% -> 0%
where the time goes in v3:
time: 47.4 us; the launch traced here: 47.2 us
  Pallas kernels  42.6 us (90%)
  local copies, waits for them, and re-layouts  2.65 us (6%)
  other arithmetic  1.28 us (3%)
  between operations  0.64 us (1%)
    pallas_call x1, Pallas kernels, local(): pl.pallas_call(kernel, out_shape=(jax.ShapeDtypeStruct((nrows, width), jn...  42.6 us
    unnamed x1, local copies, waits for them, and re-layouts  2.65 us
    mul x1, other arithmetic, local(): projected = total * (1.0 / (nrows * mesh_count * col_count))  1.28 us

profile of v3, /device:TPU:1, one launch (start us, length us, event | category | flops | bytes accessed | tf_op | source)
XLA Modules:
  0.0 47.2 jit_solution(13899486944166998090)
XLA Ops:
  0.6 42.6 %shard_map.68 = (bf16[1536,512]{1,0:T(8,128)(2,1)}, f32[8,64]{1,0:T(8,128)}) custom-call(bf16[1536,512]{1,0:T(8,128)(2,1)} %basis_ref.1, bf16[24,8,64,64]{3,2,1,0:T(8,128)(2,1)} %jac_ref.1, s32[8,24]{1,0:T(8,128)} %bitcast.3, s32[24]{0:T(128)} %live_ref.1, f32[12,128]{1,0:T(8,128)} %bitcast.2), custom_call_target="tpu_custom_call" | custom-call | tf_op jit(solution)/shard_map/pallas_call | solution.py:225
  43.3 1.3 %broadcast_multiply_fusion = f32[8,64]{1,0:T(8,128)} fusion(f32[8,64]{1,0:T(8,128)} %get-tuple-element.5), kind=kLoop, calls=%fused_computation | loop fusion | flops 512 | bytes 4096 | tf_op jit(solution)/shard_map/mul | solution.py:262
  44.5 2.7 %copy.8 = bf16[1536,512]{1,0:T(8,128)(2,1)} copy(bf16[1536,512]{1,0:T(8,128)(2,1)} %get-tuple-element.8) | data formatting | bytes 3145728

commit v4 on v3

--- a/solution.py
+++ b/solution.py
@@ -12,6 +12,7 @@
 MESH = pl.DeviceIdType.MESH
 NCORE, NX, NY, NZH = 2, 4, 4, 2
 PIECES = 4
+WRITES = 6
 
 
 def hops(step, size):
@@ -26,7 +27,7 @@
 def kernel(
     basis_ref, jac_ref, cols_ref, live_ref, acc_ref, image_ref, total_ref,
     pad, jac, cols, live, gain, top, rest, part, pair_out, pair_in, plane_out, plane_in, line_out, line_in,
-    local_sem, halo_send, halo_recv, s0, r0, s1, r1, s2, r2,
+    local_sem, jac_sem, basis_sem, halo_send, halo_recv, s0, r0, s1, r1, s2, r2,
 ):
     m, c = lax.axis_index("mesh"), lax.axis_index("col")
     nm, nc = lax.axis_size("mesh"), lax.axis_size("col")
@@ -43,6 +44,8 @@
     reach = REACH * bs
     span = GROUP * bs + 2 * reach
     lanes = 2 * bs
+    step = GROUP * bs
+    ngroup = nblk // GROUP
     rows = total_ref.shape[0]
     wide = total_ref.shape[1]
 
@@ -63,11 +66,23 @@
         pltpu.make_async_copy(cols_ref, cols, local_sem.at[0]),
         pltpu.make_async_copy(live_ref, live, local_sem.at[1]),
         pltpu.make_async_copy(acc_ref, gain, local_sem.at[2]),
-        pltpu.make_async_copy(jac_ref, jac, local_sem.at[3]),
-        pltpu.make_async_copy(basis_ref, pad.at[pl.ds(reach, nrows)], local_sem.at[4]),
     ]
+
+    def jac_move(g):
+        part_of = pl.ds(g * GROUP, GROUP)
+        return pltpu.make_async_copy(jac_ref.at[part_of], jac.at[part_of], jac_sem.at[g])
+
+    def basis_move(g):
+        return pltpu.make_async_copy(
+            basis_ref.at[pl.ds(g * step, step)], pad.at[pl.ds(reach + g * step, step)], basis_sem.at[g]
+        )
+
     for move in moves:
         move.start()
+    for g in range(ngroup):
+        jac_move(g).start()
+    for g in range(ngroup):
+        basis_move(g).start()
 
     barrier = pltpu.get_barrier_semaphore()
     peers = [low_peer, high_peer] + [line_peer(k)[1] for k in line_steps]
@@ -75,7 +90,7 @@
     for peer in peers:
         pl.semaphore_signal(barrier, inc=1, device_id=peer, device_id_type=MESH)
 
-    for move in moves[:4]:
+    for move in moves:
         move.wait()
 
     first = index * nblk
@@ -84,6 +99,7 @@
     row = lax.broadcasted_iota(jnp.int32, (bs, lanes), 0)
 
     def build(g, carry):
+        jac_move(g).wait()
         for i in range(GROUP):
             r = g * GROUP + i
             own = first + r
@@ -115,9 +131,9 @@
                     rest[here] = jnp.zeros((bs, lanes), jnp.bfloat16)
         return carry
 
-    ngroup = nblk // GROUP
     lax.fori_loop(0, ngroup, build, 0)
-    moves[4].wait()
+    for g in range(ngroup):
+        basis_move(g).wait()
 
     pl.semaphore_wait(barrier, len(peers))
     up = pltpu.make_async_remote_copy(
@@ -130,8 +146,6 @@
     )
     up.start()
     down.start()
-
-    step = GROUP * bs
 
     def apply(g, carry):
         at = pl.multiple_of(g * step, step)
@@ -213,6 +227,23 @@
         copy.wait_send()
 
 
+def finish(scale, image_ref, total_ref, image_out, projected_out, scaled, sem):
+    size = image_ref.shape[0] // WRITES
+    writes = [
+        pltpu.make_async_copy(
+            image_ref.at[pl.ds(q * size, size)], image_out.at[pl.ds(q * size, size)], sem.at[q]
+        )
+        for q in range(WRITES)
+    ]
+    for write in writes:
+        write.start()
+    scaled[...] = total_ref[...] * scale
+    small = pltpu.make_async_copy(scaled, projected_out, sem.at[WRITES])
+    small.start()
+    for write in writes + [small]:
+        write.wait()
+
+
 def local(basis, jac_blocks, block_cols, live_slots, accumulation):
     nrows, width = basis.shape
     nblk, slots, bs, _ = jac_blocks.shape
@@ -225,8 +256,8 @@
     image, total = pl.pallas_call(
         kernel,
         out_shape=(
-            jax.ShapeDtypeStruct((nrows, width), jnp.bfloat16),
-            jax.ShapeDtypeStruct((rows, wide), jnp.float32),
+            pltpu.VMEM((nrows, width), jnp.bfloat16),
+            pltpu.VMEM((rows, wide), jnp.float32),
         ),
         in_specs=[pl.BlockSpec(memory_space=pl.ANY)] * 5,
         out_specs=(pl.BlockSpec(memory_space=pltpu.VMEM), pl.BlockSpec(memory_space=pltpu.VMEM)),
@@ -245,7 +276,9 @@
             pltpu.VMEM((nplane - 1, NZH * rows, width), jnp.bfloat16),
             pltpu.VMEM((nline, rows, wide), jnp.float32),
             pltpu.VMEM((nline - 1, rows, wide), jnp.float32),
-            pltpu.SemaphoreType.DMA((5,)),
+            pltpu.SemaphoreType.DMA((3,)),
+            pltpu.SemaphoreType.DMA((ngroup,)),
+            pltpu.SemaphoreType.DMA((ngroup,)),
             pltpu.SemaphoreType.DMA((2,)),
             pltpu.SemaphoreType.DMA((2,)),
             pltpu.SemaphoreType.DMA((PIECES,)),
@@ -259,8 +292,18 @@
             collective_id=0, has_side_effects=True, vmem_limit_bytes=56 << 20
         ),
     )(basis, jac_blocks, block_cols.T, live_slots, accumulation.reshape(nrows // lanes, lanes))
-    projected = total * (1.0 / (nrows * mesh_count * col_count))
-    return (image, projected)
+    image = pltpu.with_memory_space_constraint(image, pltpu.VMEM)
+    total = pltpu.with_memory_space_constraint(total, pltpu.VMEM)
+    return pl.pallas_call(
+        functools.partial(finish, 1.0 / (nrows * mesh_count * col_count)),
+        out_shape=(
+            jax.ShapeDtypeStruct((nrows, width), jnp.bfloat16),
+            jax.ShapeDtypeStruct((rows, wide), jnp.float32),
+        ),
+        in_specs=[pl.BlockSpec(memory_space=pltpu.VMEM)] * 2,
+        out_specs=(pl.BlockSpec(memory_space=pl.ANY), pl.BlockSpec(memory_space=pl.ANY)),
+        scratch_shapes=[pltpu.VMEM((rows, wide), jnp.float32), pltpu.SemaphoreType.DMA((WRITES + 1,))],
+    )(image, total)
 
 
 def solution(mesh):

time: 47.4 us -> 43.5 us (0.918)
  local copies, waits for them, and re-layouts: 2.65 us -> 0 us
  other arithmetic: 1.28 us -> 0 us
    unnamed x1 -> x0, local copies, waits for them, and re-layouts: 2.65 us -> none
    mul x1 -> x0, other arithmetic: 1.28 us -> none  [local(): projected = total * (1.0 / (nrows * mesh_count * col_count))]
    pallas_call x1 -> x2, Pallas kernels: 42.6 us -> 42.8 us  [the longest x1 41.6 us: local(): pl.pallas_call(kernel, out_shape=(pltpu.VMEM((nrows, width), jnp.bfloat16...]
where the time goes in v4:
time: 43.5 us; the launch traced here: 43.4 us
  Pallas kernels  42.8 us (98%)
  between operations  0.64 us (1%)
    pallas_call x1, Pallas kernels, local(): pl.pallas_call(kernel, out_shape=(pltpu.VMEM((nrows, width), jnp.bfloat16...  41.6 us
    pallas_call x1, Pallas kernels, local(): pl.pallas_call(functools.partial(finish, 1.0 / (nrows * mesh_count * col_...  1.2 us

profile of v4, /device:TPU:1, one launch (start us, length us, event | category | flops | bytes accessed | tf_op | source)
XLA Modules:
  0.0 43.4 jit_solution(5115361718184009665)
XLA Ops:
  0.6 41.6 %shard_map.68 = (bf16[1536,512]{1,0:T(8,128)(2,1)S(1)}, f32[8,64]{1,0:T(8,128)S(1)}) custom-call(bf16[1536,512]{1,0:T(8,128)(2,1)} %basis_ref.1, bf16[24,8,64,64]{3,2,1,0:T(8,128)(2,1)} %jac_ref.1, s32[8,24]{1,0:T(8,128)} %bitcast.3, s32[24]{0:T(128)} %live_ref.1, f32[12,128]{1,0:T(8,128)} %bitcast.2), custom_call_target="tpu_custom_call" | custom-call | tf_op jit(solution)/shard_map/pallas_call | solution.py:256
  42.2 1.2 %shard_map.69 = (bf16[1536,512]{1,0:T(8,128)(2,1)}, f32[8,64]{1,0:T(8,128)}) custom-call(bf16[1536,512]{1,0:T(8,128)(2,1)S(1)} %get-tuple-element.4.image_ref, f32[8,64]{1,0:T(8,128)S(1)} %get-tuple-element.5.total_ref), custom_call_target="tpu_custom_call" | custom-call | tf_op jit(solution)/shard_map/pallas_call | solution.py:297

commit v5 on v4

--- a/solution.py
+++ b/solution.py
@@ -13,6 +13,7 @@
 NCORE, NX, NY, NZH = 2, 4, 4, 2
 PIECES = 4
 WRITES = 6
+FAR = (1, 2, 4)
 
 
 def hops(step, size):
@@ -27,7 +28,7 @@
 def kernel(
     basis_ref, jac_ref, cols_ref, live_ref, acc_ref, image_ref, total_ref,
     pad, jac, cols, live, gain, top, rest, part, pair_out, pair_in, plane_out, plane_in, line_out, line_in,
-    local_sem, jac_sem, basis_sem, halo_send, halo_recv, s0, r0, s1, r1, s2, r2,
+    local_sem, jac_sem, basis_sem, halo_send, halo_recv, known, s0, r0, s1, r1, s2, r2,
 ):
     m, c = lax.axis_index("mesh"), lax.axis_index("col")
     nm, nc = lax.axis_size("mesh"), lax.axis_size("col")
@@ -79,14 +80,16 @@
 
     for move in moves:
         move.start()
-    for g in range(ngroup):
-        jac_move(g).start()
+    inner = ngroup - 2
+    jac_move(1).start()
     for g in range(ngroup):
         basis_move(g).start()
+    for g in [*range(2, ngroup - 1), 0, ngroup - 1]:
+        jac_move(g).start()
 
     barrier = pltpu.get_barrier_semaphore()
-    peers = [low_peer, high_peer] + [line_peer(k)[1] for k in line_steps]
-    peers += [plane_peer(step)[1] for step in PLANE[:-1]] + [pair]
+    beside = [line_peer(1)[1], line_peer(nline - 1)[1]]
+    peers = [low_peer, high_peer] + beside + [plane_peer(step)[1] for step in PLANE[:-1]] + [pair]
     for peer in peers:
         pl.semaphore_signal(barrier, inc=1, device_id=peer, device_id_type=MESH)
 
@@ -98,8 +101,7 @@
     lane = lax.broadcasted_iota(jnp.int32, (bs, lanes), 1)
     row = lax.broadcasted_iota(jnp.int32, (bs, lanes), 0)
 
-    def build(g, carry):
-        jac_move(g).wait()
+    def build(g):
         for i in range(GROUP):
             r = g * GROUP + i
             own = first + r
@@ -129,13 +131,13 @@
                 else:
                     top[here] = jnp.zeros((bs, lanes), jnp.bfloat16)
                     rest[here] = jnp.zeros((bs, lanes), jnp.bfloat16)
-        return carry
-
-    lax.fori_loop(0, ngroup, build, 0)
+
+    jac_move(1).wait()
+    build(1)
     for g in range(ngroup):
         basis_move(g).wait()
-
-    pl.semaphore_wait(barrier, len(peers))
+    part[...] = jnp.zeros_like(part)
+
     up = pltpu.make_async_remote_copy(
         src_ref=pad.at[pl.ds(nrows, reach)], dst_ref=pad.at[pl.ds(0, reach)],
         send_sem=halo_send.at[0], recv_sem=halo_recv.at[0], device_id=high_peer, device_id_type=MESH,
@@ -144,30 +146,66 @@
         src_ref=pad.at[pl.ds(reach, reach)], dst_ref=pad.at[pl.ds(reach + nrows, reach)],
         send_sem=halo_send.at[1], recv_sem=halo_recv.at[1], device_id=low_peer, device_id_type=MESH,
     )
-    up.start()
-    down.start()
-
-    def apply(g, carry):
+    meet_at = inner * jnp.where((z == 0) | (z == nline - 1), 1, 0)
+
+    def tell(k):
+        for peer in (line_peer(FAR[k])[1], line_peer(nline - FAR[k])[1]):
+            pl.semaphore_signal(known.at[k], inc=1, device_id=peer, device_id_type=MESH)
+
+    def hear(k):
+        pl.semaphore_wait(known.at[k], 2)
+
+    far_low = jnp.where(c == 0, 1, 0)
+
+    def ends(k):
+        return jnp.where(k == inner + far_low, 1, 0), jnp.where(k == inner + 1 - far_low, 1, 0)
+
+    def order(k):
+        low_now, high_now = ends(k)
+        return (1 - low_now - high_now) * (k + 1) + high_now * (ngroup - 1)
+
+    def ready(k):
+        low_now, high_now = ends(k)
+
+        @pl.when(k == meet_at)
+        def _():
+            pl.semaphore_wait(barrier, len(peers))
+            up.start()
+            down.start()
+            tell(0)
+
+        @pl.when(low_now == 1)
+        def _():
+            up.wait_recv()
+
+        @pl.when(high_now == 1)
+        def _():
+            down.wait_recv()
+
+    def multiply(g):
         at = pl.multiple_of(g * step, step)
         window = pad[pl.ds(at, span), :]
         out = jnp.dot(top[g], window, preferred_element_type=jnp.float32)
         out += jnp.dot(rest[g], window, preferred_element_type=jnp.float32)
-        image_ref[pl.ds(at, step), :] = out.astype(image_ref.dtype)
+        out = out.astype(image_ref.dtype)
+        image_ref[pl.ds(at, step), :] = out
+        part[...] += lax.dot_general(
+            pad[pl.ds(reach + at, step), :], out, (((0,), (0,)), ((), ())), preferred_element_type=jnp.float32
+        )
+
+    def both(k, carry):
+        ready(k)
+        later = order(k + 1)
+        jac_move(later).wait()
+        multiply(order(k))
+        build(later)
         return carry
 
-    def project(start, size):
-        return lax.dot_general(
-            pad[pl.ds(reach + start, size), :], image_ref[pl.ds(start, size), :],
-            (((0,), (0,)), ((), ())), preferred_element_type=jnp.float32,
-        )
-
-    lax.fori_loop(1, ngroup - 1, apply, 0)
-    part[...] = project(step, nrows - 2 * step)
-    up.wait()
-    down.wait()
-    apply(0, 0)
-    apply(ngroup - 1, 0)
-    part[...] += project(0, step) + project(nrows - step, step)
+    lax.fori_loop(0, ngroup - 1, both, 0)
+    hear(0)
+    tell(1)
+    ready(ngroup - 1)
+    multiply(order(ngroup - 1))
 
     def share(j, which):
         at = [pl.multiple_of(((h * nplane + j) * NCORE + which) * rows, rows) for h in range(NZH)]
@@ -185,6 +223,8 @@
         swap.start()
         swaps.append(swap)
 
+    hear(1)
+    tell(2)
     sent = []
     acc = None
     for q in range(PIECES):
@@ -209,6 +249,7 @@
     for h in range(NZH):
         for q in range(nc):
             line_out[h * nc + q] = acc[h * rows:(h + 1) * rows, q * wide:(q + 1) * wide]
+    hear(2)
     last = []
     for n, k in enumerate(line_steps):
         j, peer = line_peer(k)
@@ -223,7 +264,7 @@
         last[n].wait_recv()
         total += line_in[n]
     total_ref[...] = total
-    for copy in swaps + sent + last:
+    for copy in [up, down] + swaps + sent + last:
         copy.wait_send()
 
 
@@ -281,6 +322,7 @@
             pltpu.SemaphoreType.DMA((ngroup,)),
             pltpu.SemaphoreType.DMA((2,)),
             pltpu.SemaphoreType.DMA((2,)),
+            pltpu.SemaphoreType.REGULAR((len(FAR),)),
             pltpu.SemaphoreType.DMA((PIECES,)),
             pltpu.SemaphoreType.DMA((PIECES,)),
             pltpu.SemaphoreType.DMA((nplane - 1,)),

time: 43.5 us -> 41.9 us (0.963)
  Pallas kernels: 42.8 us -> 41.1 us
    pallas_call x1, Pallas kernels: 41.6 us -> 39.9 us  [local(): pl.pallas_call(kernel, out_shape=(pltpu.VMEM((nrows, width), jnp.bfloat16...]
where the time goes in v5:
time: 41.9 us; the launch traced here: 41.8 us
  Pallas kernels  41.1 us (98%)
  between operations  0.64 us (2%)
    pallas_call x1, Pallas kernels, local(): pl.pallas_call(kernel, out_shape=(pltpu.VMEM((nrows, width), jnp.bfloat16...  39.9 us
    pallas_call x1, Pallas kernels, local(): pl.pallas_call(functools.partial(finish, 1.0 / (nrows * mesh_count * col_...  1.2 us

profile of v5, /device:TPU:1, one launch (start us, length us, event | category | flops | bytes accessed | tf_op | source)
XLA Modules:
  0.0 41.8 jit_solution(11841203051505193396)
XLA Ops:
  0.6 39.9 %shard_map.68 = (bf16[1536,512]{1,0:T(8,128)(2,1)S(1)}, f32[8,64]{1,0:T(8,128)S(1)}) custom-call(bf16[1536,512]{1,0:T(8,128)(2,1)} %basis_ref.1, bf16[24,8,64,64]{3,2,1,0:T(8,128)(2,1)} %jac_ref.1, s32[8,24]{1,0:T(8,128)} %bitcast.3, s32[24]{0:T(128)} %live_ref.1, f32[12,128]{1,0:T(8,128)} %bitcast.2), custom_call_target="tpu_custom_call" | custom-call | tf_op jit(solution)/shard_map/pallas_call | solution.py:297
  40.6 1.2 %shard_map.69 = (bf16[1536,512]{1,0:T(8,128)(2,1)}, f32[8,64]{1,0:T(8,128)}) custom-call(bf16[1536,512]{1,0:T(8,128)(2,1)S(1)} %get-tuple-element.4.image_ref, f32[8,64]{1,0:T(8,128)S(1)} %get-tuple-element.5.total_ref), custom_call_target="tpu_custom_call" | custom-call | tf_op jit(solution)/shard_map/pallas_call | solution.py:339

commit v6 on v5

--- a/solution.py
+++ b/solution.py
@@ -170,8 +170,16 @@
         @pl.when(k == meet_at)
         def _():
             pl.semaphore_wait(barrier, len(peers))
-            up.start()
-            down.start()
+            @pl.when(far_low == 1)
+            def _():
+                down.start()
+                up.start()
+
+            @pl.when(far_low == 0)
+            def _():
+                up.start()
+                down.start()
+
             tell(0)
 
         @pl.when(low_now == 1)
@@ -223,8 +231,6 @@
         swap.start()
         swaps.append(swap)
 
-    hear(1)
-    tell(2)
     sent = []
     acc = None
     for q in range(PIECES):
@@ -242,6 +248,8 @@
             )
             copy.start()
             sent.append(copy)
+    hear(1)
+    tell(2)
     for n in reversed(range(nplane - 1)):
         sent[n].wait_recv()
         acc += plane_in[n].astype(jnp.float32)

time: 41.9 us -> 41.7 us (level)
  no operation moved by 1% of the time
where the time goes in v6:
time: 41.7 us; the launch traced here: 41.6 us
  Pallas kernels  41 us (98%)
  between operations  0.64 us (2%)
    pallas_call x1, Pallas kernels, local(): pl.pallas_call(kernel, out_shape=(pltpu.VMEM((nrows, width), jnp.bfloat16...  39.8 us
    pallas_call x1, Pallas kernels, local(): pl.pallas_call(functools.partial(finish, 1.0 / (nrows * mesh_count * col_...  1.2 us

profile of v6, /device:TPU:1, one launch (start us, length us, event | category | flops | bytes accessed | tf_op | source)
XLA Modules:
  0.0 41.6 jit_solution(16355644123005942619)
XLA Ops:
  0.6 39.8 %shard_map.68 = (bf16[1536,512]{1,0:T(8,128)(2,1)S(1)}, f32[8,64]{1,0:T(8,128)S(1)}) custom-call(bf16[1536,512]{1,0:T(8,128)(2,1)} %basis_ref.1, bf16[24,8,64,64]{3,2,1,0:T(8,128)(2,1)} %jac_ref.1, s32[8,24]{1,0:T(8,128)} %bitcast.3, s32[24]{0:T(128)} %live_ref.1, f32[12,128]{1,0:T(8,128)} %bitcast.2), custom_call_target="tpu_custom_call" | custom-call | tf_op jit(solution)/shard_map/pallas_call | solution.py:305
  40.4 1.2 %shard_map.69 = (bf16[1536,512]{1,0:T(8,128)(2,1)}, f32[8,64]{1,0:T(8,128)}) custom-call(bf16[1536,512]{1,0:T(8,128)(2,1)S(1)} %get-tuple-element.4.image_ref, f32[8,64]{1,0:T(8,128)S(1)} %get-tuple-element.5.total_ref), custom_call_target="tpu_custom_call" | custom-call | tf_op jit(solution)/shard_map/pallas_call | solution.py:347
